TPU v7x, 32 devices: a whole 2x2x4 slice. The times are simulated.
32 devices in a mesh: row: 8 (over z, x), col: 4 (over y, core).
Axes of the slice: x: 2, y: 2, z: 4, core: 2. Of those that a mesh axis runs over, the one named last changes fastest.
Arguments:
- features: bfloat16 [14336, 2048], P('row', 'col'), may hold values from -6 to 6
- neighbours: int32 [14336, 32], P('row'), may hold values from -1 to 127, as said below
- node_valid: int32 [14336], P('row'), may hold values from 0 to 1, as said below
- weight_one: bfloat16 [2048, 2048], P(None, 'col'), may hold values from -0.125 to 0.125
- gamma_one: float32 [2048], P('col'), may hold values from 0.25 to 1.75
- beta_one: float32 [2048], P('col'), may hold values from -0.5 to 0.5
- weight_two: bfloat16 [2048, 2048], P(None, 'col'), may hold values from -0.125 to 0.125
- gamma_two: float32 [2048], P('col'), may hold values from 0.25 to 1.75
- beta_two: float32 [2048], P('col'), may hold values from -0.5 to 0.5
- cotangent: bfloat16 [14336, 2048], P('row', 'col'), may hold values from -6 to 6
Outputs:
- output: float32 [14336, 2048], P('row', 'col')
- grad_features: float32 [14336, 2048], P('row', 'col')
- grad_weight_one: float32 [2048, 2048], P(None, 'col')
- grad_gamma_one: float32 [2048], P('col')
- grad_beta_one: float32 [2048], P('col')
- grad_weight_two: float32 [2048, 2048], P(None, 'col')
- grad_gamma_two: float32 [2048], P('col')
- grad_beta_two: float32 [2048], P('col')
Inputs may be any that keep to these rules, and one draw needn't show every extreme that they name: `neighbours`: entries >= 0 name valid nodes of the same slot; every valid node has 1 to 32 such entries, first in its list, the rest are -1; a padding row has only -1; some slot is full. `node_valid`: in each slot the valid nodes come first and number at least 40.
All inputs are finite; a program needn't handle non-finite values.
Results may differ from a plain program's by a relative error of at most 0.012.
Values may be sent and summed in bfloat16 or wider, within the bound.
No kernel may reach another device: no remote copies, remote signals or barrier semaphores. Data moves between devices by JAX's collectives and lax.ppermute only.
A program may use at most 128 MiB of HBM per device.

v0:
```python
import jax
import jax.numpy as jnp
from jax import lax
from jax.sharding import PartitionSpec as P

SLOT = 128
NBR = 32
EPSILON = 1e-05


def build_tiles(neighbours):
    entries_all = neighbours.reshape(-1, SLOT, NBR)

    def build(entries):
        columns = jnp.arange(SLOT, dtype=jnp.int32)
        hits = jnp.sum((entries[:, :, None] == columns[None, None, :]).astype(jnp.float32), axis=1)
        degree = jnp.sum((entries >= 0).astype(jnp.float32), axis=1)
        joined = hits + jnp.eye(SLOT, dtype=jnp.float32)
        return joined / (degree[:, None] + 1.0)

    tiles = lax.map(build, entries_all)
    return (tiles, jnp.diagonal(tiles, axis1=1, axis2=2))


def spread(values, tiles, self_weight):
    shaped = values.reshape(tiles.shape[0], SLOT, values.shape[1])
    summed = jnp.einsum("sij,sjd->sid", tiles, shaped, precision=lax.Precision.HIGHEST)
    return (summed + self_weight[:, :, None] * shaped).reshape(values.shape)


def spread_back(grads, tiles, self_weight):
    shaped = grads.reshape(tiles.shape[0], SLOT, grads.shape[1])
    summed = jnp.einsum("sji,sjd->sid", tiles, shaped, precision=lax.Precision.HIGHEST)
    return (summed + self_weight[:, :, None] * shaped).reshape(grads.shape)


def moments(linear, valid):
    total_valid, summed = lax.psum((jnp.sum(valid), jnp.sum(valid * linear, axis=0)), "row")
    mean = summed / total_valid
    centred = linear - mean
    variance = lax.psum(jnp.sum(valid * centred * centred, axis=0), "row") / total_valid
    return (total_valid, mean, variance)


def forward_layer(values, weight, gamma, beta, tiles, self_weight, valid):
    mixed = spread(values, tiles, self_weight).astype(jnp.bfloat16)
    gathered = lax.all_gather(mixed, "col", axis=1, tiled=True)
    linear = jnp.dot(gathered, weight, preferred_element_type=jnp.float32)
    total_valid, mean, variance = moments(linear, valid)
    inv_std = lax.rsqrt(variance + EPSILON)
    normed = (linear - mean) * inv_std
    before = gamma * normed + beta
    result = valid * jax.nn.silu(before)
    return (result, (gathered, normed, inv_std, before, total_valid))


def backward_layer(grad_result, weight, gamma, kept, tiles, self_weight, valid):
    gathered, normed, inv_std, before, total_valid = kept
    sigmoid_value = jax.nn.sigmoid(before)
    slope = sigmoid_value * (1.0 + before * (1.0 - sigmoid_value))
    grad_before = grad_result * valid * slope
    grad_beta, grad_gamma = lax.psum(
        (jnp.sum(grad_before, axis=0), jnp.sum(grad_before * normed, axis=0)), "row"
    )
    grad_normed = gamma * grad_before
    grad_linear = inv_std * (
        grad_normed - valid * (gamma * grad_beta + normed * gamma * grad_gamma) / total_valid
    )
    grad_low = grad_linear.astype(jnp.bfloat16)
    weight_terms = lax.dot_general(
        gathered, grad_low, (((0,), (0,)), ((), ())), preferred_element_type=jnp.float32
    )
    grad_weight = lax.psum(weight_terms, "row")
    partial_terms = lax.dot_general(
        grad_low, weight, (((1,), (1,)), ((), ())), preferred_element_type=jnp.float32
    )
    grad_mixed = lax.psum_scatter(partial_terms, "col", scatter_dimension=1, tiled=True)
    grad_values = spread_back(grad_mixed, tiles, self_weight)
    return (grad_values, grad_weight, grad_gamma, grad_beta)


def local(
    features,
    neighbours,
    node_valid,
    weight_one,
    gamma_one,
    beta_one,
    weight_two,
    gamma_two,
    beta_two,
    cotangent,
):
    tiles, self_weight = build_tiles(neighbours)
    valid = node_valid.astype(jnp.float32)[:, None]
    hidden, kept_one = forward_layer(
        features.astype(jnp.float32), weight_one, gamma_one, beta_one, tiles, self_weight, valid
    )
    output, kept_two = forward_layer(
        hidden, weight_two, gamma_two, beta_two, tiles, self_weight, valid
    )
    grad_hidden, grad_weight_two, grad_gamma_two, grad_beta_two = backward_layer(
        cotangent.astype(jnp.float32), weight_two, gamma_two, kept_two, tiles, self_weight, valid
    )
    grad_features, grad_weight_one, grad_gamma_one, grad_beta_one = backward_layer(
        grad_hidden, weight_one, gamma_one, kept_one, tiles, self_weight, valid
    )
    return (
        output,
        grad_features,
        grad_weight_one,
        grad_gamma_one,
        grad_beta_one,
        grad_weight_two,
        grad_gamma_two,
        grad_beta_two,
    )


def solution(mesh):
    placed = (
        P("row", "col"),
        P("row", None),
        P("row"),
        P(None, "col"),
        P("col"),
        P("col"),
        P(None, "col"),
        P("col"),
        P("col"),
        P("row", "col"),
    )
    return jax.shard_map(
        local,
        mesh=mesh,
        in_specs=placed,
        out_specs=(
            P("row", "col"),
            P("row", "col"),
            P(None, "col"),
            P("col"),
            P("col"),
            P(None, "col"),
            P("col"),
            P("col"),
        ),
        check_vma=False,
    )
```

profile of v0, /device:TPU:0, one launch (start us, length us, event | category | flops | bytes accessed | tf_op | source)
XLA Modules:
  0.0 855.5 jit_solution(2408295498759646820)
XLA Ops:
  7.3 2.3 copy.23
  9.6 27.6 %while.10 = (s32[]{:T(128)}, f32[14,128,128]{2,1,0:T(8,128)S(1)}, s32[14,128,32]{2,1,0:T(8,128)}, s32[]{:T(128)}) while((s32[]{:T(128)}, f32[14,128,128]{2,1,0:T(8,128)S(1)}, s32[14,128,32]{2,1,0:T(8,128)}, s32[]{:T(128)}) %tuple.47), condition=%wide.region_3.4_spmd, body=%wide.region_0.3_spmd.sunk | while | flops 1634306 | bytes 247877 | solution.py:21
  37.2 4.7 copy.24
  43.7 5.1 add_convert_fusion.1
  49.5 54.5 %all-gather.3.cloned.1.call-done = bf16[1792,2048]{1,0:T(8,128)(2,1)} async-done(((bf16[1792,512]{1,0:T(8,128)(2,1)}), bf16[1792,2048]{1,0:T(8,128)(2,1)}) %all-gather.3.cloned.1.call-update) | async-done | bytes 7340048 | tf_op jit(solution)/shard_map/all_gather | solution.py:47
  104.0 9.5 %multiply_reduce_fusion.3 = (f32[512]{0:T(512)S(1)}, f32[1792,512]{1,0:T(8,128)}) fusion(f32[1792]{0:T(1024)S(1)} %convert_element_type.41, bf16[1792,2048]{1,0:T(8,128)(2,1)} %all-gather.3.cloned.1.call-done, bf16[2048,512]{1,0:T(8,128)(2,1)} %param.15), kind=kOutput, calls=%fused_computation.29 | convolution fusion | flops 3759930880 | bytes 13116416 | tf_op jit(solution)/shard_map/dot_general | solution.py:48
  113.5 22.0 %all-reduce.2 = (f32[512]{0:T(512)S(1)}, f32[]{:T(128)}) all-reduce(f32[512]{0:T(512)S(1)} %get-tuple-element.49, f32[]{:T(128)} %convert_reduce_fusion.2), channel_id=1, replica_groups=mesh['row'=8,'col'=4] {'row'}, use_global_device_ids=true, to_apply=%region_5.6 | all-reduce | flops 513 | bytes 4104 | tf_op jit(solution)/shard_map/psum | solution.py:38
  136.0 2.6 fusion.2
  138.6 17.1 %psum.82 = f32[512]{0:T(512)S(1)} all-reduce(f32[512]{0:T(512)S(1)} %fusion.2), channel_id=1, replica_groups=mesh['row'=8,'col'=4] {'row'}, use_global_device_ids=true, to_apply=%region_9.10 | all-reduce | flops 512 | bytes 4096 | tf_op jit(solution)/shard_map/psum | solution.py:41
  156.3 3.0 multiply_multiply_fusion.4
  159.4 4.5 add_convert_fusion
  164.1 50.0 %all-gather.5.cloned.1.call-done = bf16[1792,2048]{1,0:T(8,128)(2,1)} async-done(((bf16[1792,512]{1,0:T(8,128)(2,1)}), bf16[1792,2048]{1,0:T(8,128)(2,1)}) %all-gather.5.cloned.1.call-update) | async-done | bytes 7340048 | tf_op jit(solution)/shard_map/all_gather | solution.py:47
  214.1 8.9 %multiply_reduce_fusion.2 = (f32[512]{0:T(512)S(1)}, f32[1792,512]{1,0:T(8,128)}) fusion(f32[1792]{0:T(1024)S(1)} %convert_element_type.41, bf16[1792,2048]{1,0:T(8,128)(2,1)} %all-gather.5.cloned.1.call-done, bf16[2048,512]{1,0:T(8,128)(2,1)S(1)} %copy-done), kind=kOutput, calls=%fused_computation.25 | convolution fusion | flops 3759930880 | bytes 13116416 | tf_op jit(solution)/shard_map/dot_general | solution.py:48
  223.0 21.5 %psum.83 = f32[512]{0:T(512)S(1)} all-reduce(f32[512]{0:T(512)S(1)} %get-tuple-element.51), channel_id=1, replica_groups=mesh['row'=8,'col'=4] {'row'}, use_global_device_ids=true, to_apply=%region_11.12 | all-reduce | flops 512 | bytes 4096 | tf_op jit(solution)/shard_map/psum | solution.py:38
  245.1 2.6 fusion.3
  247.7 17.1 %psum.84 = f32[512]{0:T(512)S(1)} all-reduce(f32[512]{0:T(512)S(1)} %fusion.3), channel_id=1, replica_groups=mesh['row'=8,'col'=4] {'row'}, use_global_device_ids=true, to_apply=%region_13.14 | all-reduce | flops 512 | bytes 4096 | tf_op jit(solution)/shard_map/psum | solution.py:41
  265.4 6.3 fusion.6
  271.7 19.1 %all-reduce.1 = (f32[512]{0:T(512)S(1)}, f32[512]{0:T(512)S(1)}) all-reduce(f32[512]{0:T(512)S(1)} %get-tuple-element.29, f32[512]{0:T(512)S(1)} %get-tuple-element.28), channel_id=1, replica_groups=mesh['row'=8,'col'=4] {'row'}, use_global_device_ids=true, to_apply=%region_17.18 | all-reduce | flops 1024 | bytes 8192 | tf_op jit(solution)/shard_map/psum | solution.py:62
  290.8 4.5 multiply_convert_fusion.1
  296.6 7.2 fusion.8
  304.1 109.0 %reduce-scatter.3.cloned.1.call-done = f32[1792,512]{1,0:T(8,128)} async-done(((f32[1792,2048]{1,0:T(8,128)}), f32[1792,512]{1,0:T(8,128)}) %reduce-scatter.3.cloned.1.call-update) | async-done | bytes 3670032 | tf_op jit(solution)/shard_map/reduce_scatter | solution.py:77
  413.1 6.8 multiply_add_fusion.1
  419.9 3.7 fusion.5
  423.7 21.3 %all-reduce = (f32[512]{0:T(512)S(1)}, f32[512]{0:T(512)S(1)}) all-reduce(f32[512]{0:T(512)S(1)} %get-tuple-element.27, f32[512]{0:T(512)S(1)} %get-tuple-element.26), channel_id=1, replica_groups=mesh['row'=8,'col'=4] {'row'}, use_global_device_ids=true, to_apply=%region_22.23 | all-reduce | flops 1024 | bytes 8192 | tf_op jit(solution)/shard_map/psum | solution.py:62
  445.0 4.7 multiply_convert_fusion
  449.8 7.3 fusion.9
  458.5 9.9 %fusion.11 = f32[2048,512]{1,0:T(8,128)} fusion(bf16[1792,2048]{1,0:T(8,128)(2,1)} %all-gather.5.cloned.1.call-done, bf16[1792,512]{1,0:T(8,128)(2,1)S(1)} %copy-done.5), kind=kOutput, calls=%fused_computation.44 | convolution fusion | flops 3758096384 | bytes 13369344 | tf_op jit(solution)/shard_map/dot_general | solution.py:70
  468.4 10.5 %fusion.10 = f32[2048,512]{1,0:T(8,128)} fusion(bf16[1792,2048]{1,0:T(8,128)(2,1)} %all-gather.3.cloned.1.call-done, bf16[1792,512]{1,0:T(8,128)(2,1)S(1)} %copy-done.7), kind=kOutput, calls=%fused_computation.43 | convolution fusion | flops 3758096384 | bytes 13369344 | tf_op jit(solution)/shard_map/dot_general | solution.py:70
  479.0 87.5 %reduce-scatter.5.cloned.1.call-done = f32[1792,512]{1,0:T(8,128)} async-done(((f32[1792,2048]{1,0:T(8,128)}), f32[1792,512]{1,0:T(8,128)}) %reduce-scatter.5.cloned.1.call-update) | async-done | bytes 3670032 | tf_op jit(solution)/shard_map/reduce_scatter | solution.py:77
  566.5 8.5 multiply_add_fusion
  575.0 267.1 %all-reduce.6.cloned.1.call-done = (f32[2048,512]{1,0:T(8,128)}, f32[2048,512]{1,0:T(8,128)}) async-done(((f32[2048,512]{1,0:T(8,128)}, f32[2048,512]{1,0:T(8,128)}), (f32[2048,512]{1,0:T(8,128)}, f32[2048,512]{1,0:T(8,128)})) %all-reduce.6.cloned.1.call-update) | async-done | bytes 8388624 | tf_op jit(solution)/shard_map/psum | solution.py:73
  842.1 4.8 copy.41
  (115 shorter events, 37.2 us)
Async XLA Ops:
  7.2 207.0 %copy-start = (bf16[2048,512]{1,0:T(8,128)(2,1)S(1)}, bf16[2048,512]{1,0:T(8,128)(2,1)}, u32[]{:S(2)}) copy-start(bf16[2048,512]{1,0:T(8,128)(2,1)} %param.18) | copy-start | bytes 6291460
  7.2 96.8 %all-gather.3.cloned.1.call-start = ((), (), s32[]{:S(2)}) async-start(), calls=%async_computation.2 | async-start | bytes 9175040 | tf_op jit(solution)/shard_map/all_gather | solution.py:47
  41.8 7.0 copy-start.8
  48.8 165.3 %all-gather.5.cloned.1.call-start = ((), (), s32[]{:S(2)}) async-start(), calls=%async_computation.3 | async-start | bytes 9175040 | tf_op jit(solution)/shard_map/all_gather | solution.py:47
  113.5 42.8 %copy-start.9 = (f32[512]{0:T(512)S(1)}, f32[512]{0:T(512)}, u32[]{:S(2)}) copy-start(f32[512]{0:T(512)} %param.16) | copy-start | bytes 6148
  113.5 42.8 %copy-start.11 = (f32[512]{0:T(512)S(1)}, f32[512]{0:T(512)}, u32[]{:S(2)}) copy-start(f32[512]{0:T(512)} %param.17) | copy-start | bytes 6148
  163.9 249.3 %reduce-scatter.3.cloned.1.call-start = ((), (), s32[]{:S(2)}) async-start(), calls=%async_computation.4 | async-start | bytes 18350080 | tf_op jit(solution)/shard_map/reduce_scatter | solution.py:77
  223.0 42.3 %copy-start.10 = (f32[512]{0:T(512)S(1)}, f32[512]{0:T(512)}, u32[]{:S(2)}) copy-start(f32[512]{0:T(512)} %param.19) | copy-start | bytes 6148
  223.0 42.3 %copy-start.12 = (f32[512]{0:T(512)S(1)}, f32[512]{0:T(512)}, u32[]{:S(2)}) copy-start(f32[512]{0:T(512)} %param.20) | copy-start | bytes 6148
  290.8 4.5 copy-start.13
  290.8 4.6 copy-start.15
  295.3 1.2 copy-start.4
  303.8 262.6 %reduce-scatter.5.cloned.1.call-start = ((), (), s32[]{:S(2)}) async-start(), calls=%async_computation.5 | async-start | bytes 18350080 | tf_op jit(solution)/shard_map/reduce_scatter | solution.py:77
  413.1 6.8 copy-start.2
  445.0 4.7 copy-start.14
  445.0 4.7 copy-start.16
  445.0 4.7 copy-start.17
  449.7 7.3 copy-start.6
  457.0 1.5 copy-start.5
  457.0 385.1 %all-reduce.6.cloned.1.call-start = ((), (), s32[]{:S(2)}) async-start(), calls=%async_computation.6 | async-start | bytes 16777216 | tf_op jit(solution)/shard_map/psum | solution.py:73
  458.5 9.9 %copy-start.7 = (bf16[1792,512]{1,0:T(8,128)(2,1)S(1)}, bf16[1792,512]{1,0:T(8,128)(2,1)}, u32[]{:S(2)}) copy-start(bf16[1792,512]{1,0:T(8,128)(2,1)} %copy-done.6) | copy-start | bytes 5505028
  842.1 4.8 copy-start.3
  842.1 6.8 copy-start.1
Sparse Core Ops, SparseCore 0:
  48.9 55.0 all-gather.2
  164.0 50.1 all-gather.4
  303.9 109.1 reduce-scatter.2
  457.2 109.2 reduce-scatter.4
  571.0 271.0 all-reduce.5
where the time goes:
time: 857 us; the launch traced here: 855 us
  waiting for transfers between devices  568 us (66%)
  blocking collectives  118 us (14%)
  matrix products  78.2 us (9%)
  other arithmetic  57.2 us (7%)
  local copies, waits for them, and re-layouts  18.1 us (2%)
  between operations  14 us (2%)
    psum x1, waiting for transfers between devices, backward_layer(): grad_weight = lax.psum(weight_terms, 'row')  267 us
    reduce_scatter x2, waiting for transfers between devices, backward_layer(): lax.psum_scatter(partial_terms, 'col', scatter_dimension=1, tiled=True)  197 us
    all_gather x2, waiting for transfers between devices, forward_layer(): gathered = lax.all_gather(mixed, 'col', axis=1, tiled=True)  105 us
    psum x2, blocking collectives, moments(): lax.psum((jnp.sum(valid), jnp.sum(valid * linear, axis=0)), 'row')  43.4 us
    psum x2, blocking collectives, backward_layer(): lax.psum((jnp.sum(grad_before, axis=0), jnp.sum(grad_before * normed, axi...  40.5 us
    psum x2, blocking collectives, moments(): lax.psum(jnp.sum(valid * centred * centred, axis=0), 'row') / total_valid  34.3 us
    dot_general x2, matrix products, backward_layer(): lax.dot_general(gathered, grad_low, (((0,), (0,)), ((), ())), preferred_e...  20.4 us
    dot_general x2, matrix products, forward_layer(): linear = jnp.dot(gathered, weight, preferred_element_type=jnp.float32)  18.4 us
  transfers between devices with their start and end apart: 5, of which 5 were waited for; matrix products, arithmetic and copies ran while one was open for 3% of the time, Pallas kernels for 0%

commit v1 on v0

--- a/solution.py
+++ b/solution.py
@@ -44,7 +44,30 @@
 
 def forward_layer(values, weight, gamma, beta, tiles, self_weight, valid):
     mixed = spread(values, tiles, self_weight).astype(jnp.bfloat16)
-    gathered = lax.all_gather(mixed, "col", axis=1, tiled=True)
+    mat_out = jax.lax.axis_size("col")
+    prior, then, a_now = (mat_out, jax.lax.axis_index("col"), mixed.shape[1])
+    pages = []
+    for idx, i in enumerate(mixed.shape):
+        pages.append(i * prior if idx == 1 else i)
+    t_next = jnp.zeros(pages, mixed.dtype)
+    gathered = lax.dynamic_update_slice_in_dim(t_next, mixed, then * a_now, axis=1)
+    inter = item_now = mixed
+    for d in range(1, prior // 2 + 1):
+        found = []
+        for idx in range(prior):
+            found.append((idx, (idx + 1) % prior))
+        inter = jax.lax.ppermute(inter, "col", found)
+        gathered = lax.dynamic_update_slice_in_dim(
+            gathered, inter, (then - d) % prior * a_now, axis=1
+        )
+        if 2 * d < prior:
+            line_up = []
+            for idx in range(prior):
+                line_up.append((idx, (idx - 1) % prior))
+            item_now = jax.lax.ppermute(item_now, "col", line_up)
+            gathered = lax.dynamic_update_slice_in_dim(
+                gathered, item_now, (then + d) % prior * a_now, axis=1
+            )
     linear = jnp.dot(gathered, weight, preferred_element_type=jnp.float32)
     total_valid, mean, variance = moments(linear, valid)
     inv_std = lax.rsqrt(variance + EPSILON)

time: 857 us -> 884 us (1.032)
  local copies, waits for them, and re-layouts: 18.1 us -> 28.6 us
  starting transfers between devices: 0.87 us -> 10.1 us
    ppermute x0 -> x6, waiting for transfers between devices: none -> 107 us  [the longest x4 107 us: forward_layer(): inter = jax.lax.ppermute(inter, 'col', found)]
    all_gather x2 -> x0, waiting for transfers between devices: 105 us -> none  [forward_layer(): gathered = lax.all_gather(mixed, 'col', axis=1, tiled=True)]
    ppermute x0 -> x6, starting transfers between devices: none -> 9.75 us  [the longest x4 6.06 us: forward_layer(): inter = jax.lax.ppermute(inter, 'col', found)]
  transfers between devices with their start and end apart: 5 -> 9, of which waited for: 5 -> 7; matrix products, arithmetic and copies ran while one was open for 3% -> 4% of each run, Pallas kernels for 0% -> 0%
where the time goes in v1:
time: 884 us; the launch traced here: 876 us
  waiting for transfers between devices  576 us (65%)
  blocking collectives  118 us (13%)
  matrix products  70.7 us (8%)
  other arithmetic  57.2 us (6%)
  local copies, waits for them, and re-layouts  28.6 us (3%)
  between operations  14.4 us (2%)
  starting transfers between devices  10.1 us (1%)
    psum x1, waiting for transfers between devices, backward_layer(): grad_weight = lax.psum(weight_terms, 'row')  267 us
    reduce_scatter x2, waiting for transfers between devices, backward_layer(): lax.psum_scatter(partial_terms, 'col', scatter_dimension=1, tiled=True)  202 us
    ppermute x4, waiting for transfers between devices, forward_layer(): inter = jax.lax.ppermute(inter, 'col', found)  107 us
    psum x2, blocking collectives, moments(): lax.psum((jnp.sum(valid), jnp.sum(valid * linear, axis=0)), 'row')  43.1 us
    psum x2, blocking collectives, backward_layer(): lax.psum((jnp.sum(grad_before, axis=0), jnp.sum(grad_before * normed, axi...  40.6 us
    psum x2, blocking collectives, moments(): lax.psum(jnp.sum(valid * centred * centred, axis=0), 'row') / total_valid  34.7 us
    dot_general x2, matrix products, backward_layer(): lax.dot_general(gathered, grad_low, (((0,), (0,)), ((), ())), preferred_e...  20.4 us
  transfers between devices with their start and end apart: 9, of which 7 were waited for; matrix products, arithmetic and copies ran while one was open for 4% of the time, Pallas kernels for 0%

profile of v1, /device:TPU:0, one launch (start us, length us, event | category | flops | bytes accessed | tf_op | source)
XLA Modules:
  0.0 875.8 jit_solution(12742616067314262111)
XLA Ops:
  9.6 27.6 %while.10 = (s32[]{:T(128)}, f32[14,128,128]{2,1,0:T(8,128)S(1)}, s32[14,128,32]{2,1,0:T(8,128)}, s32[]{:T(128)}) while((s32[]{:T(128)}, f32[14,128,128]{2,1,0:T(8,128)S(1)}, s32[14,128,32]{2,1,0:T(8,128)}, s32[]{:T(128)}) %tuple.43), condition=%wide.region_3.4_spmd, body=%wide.region_0.3_spmd.sunk | while | flops 1634306 | bytes 247877 | solution.py:21
  37.2 4.7 copy.24
  43.7 5.1 add_convert_fusion.1
  51.2 38.2 %collective-permute-done = bf16[1792,512]{1,0:T(8,128)(2,1)} collective-permute-done((bf16[1792,512]{1,0:T(8,128)(2,1)}, bf16[1792,512]{1,0:T(8,128)(2,1)}, u32[]{:S(2)}, u32[]{:S(2)}) %collective-permute-start) | collective-permute-done | bytes 1835040 | tf_op jit(solution)/shard_map/ppermute | solution.py:59
  99.1 13.2 %collective-permute-done.2 = bf16[1792,512]{1,0:T(8,128)(2,1)} collective-permute-done((bf16[1792,512]{1,0:T(8,128)(2,1)}, bf16[1792,512]{1,0:T(8,128)(2,1)}, u32[]{:S(2)}, u32[]{:S(2)}) %collective-permute-start.2) | collective-permute-done | bytes 1835040 | tf_op jit(solution)/shard_map/ppermute | solution.py:59
  114.2 5.8 multiply_reduce_fusion.3
  120.0 23.9 %all-reduce.2 = (f32[512]{0:T(512)S(1)}, f32[]{:T(128)}) all-reduce(f32[512]{0:T(512)S(1)} %get-tuple-element.49, f32[]{:T(128)} %convert_reduce_fusion.2), channel_id=1, replica_groups=mesh['row'=8,'col'=4] {'row'}, use_global_device_ids=true, to_apply=%region_5.6 | all-reduce | flops 513 | bytes 4104 | tf_op jit(solution)/shard_map/psum | solution.py:38
  147.0 17.6 %psum.82 = f32[512]{0:T(512)S(1)} all-reduce(f32[512]{0:T(512)S(1)} %fusion.2), channel_id=1, replica_groups=mesh['row'=8,'col'=4] {'row'}, use_global_device_ids=true, to_apply=%region_9.10 | all-reduce | flops 512 | bytes 4096 | tf_op jit(solution)/shard_map/psum | solution.py:41
  165.2 3.0 multiply_multiply_fusion.4
  168.2 3.8 add_convert_fusion
  173.8 37.6 %collective-permute-done.3 = bf16[1792,512]{1,0:T(8,128)(2,1)S(1)} collective-permute-done((bf16[1792,512]{1,0:T(8,128)(2,1)S(1)}, bf16[1792,512]{1,0:T(8,128)(2,1)S(1)}, u32[]{:S(2)}, u32[]{:S(2)}) %collective-permute-start.3) | collective-permute-done | bytes 1835040 | tf_op jit(solution)/shard_map/ppermute | solution.py:59
  211.4 3.0 collective-permute-start.5
  216.2 17.8 %collective-permute-done.5 = bf16[1792,512]{1,0:T(8,128)(2,1)S(1)} collective-permute-done((bf16[1792,512]{1,0:T(8,128)(2,1)S(1)}, bf16[1792,512]{1,0:T(8,128)(2,1)S(1)}, u32[]{:S(2)}, u32[]{:S(2)}) %collective-permute-start.5) | collective-permute-done | bytes 1835040 | tf_op jit(solution)/shard_map/ppermute | solution.py:59
  234.4 5.8 multiply_reduce_fusion.2
  240.2 19.3 %psum.83 = f32[512]{0:T(512)S(1)} all-reduce(f32[512]{0:T(512)S(1)} %get-tuple-element.51), channel_id=1, replica_groups=mesh['row'=8,'col'=4] {'row'}, use_global_device_ids=true, to_apply=%region_11.12 | all-reduce | flops 512 | bytes 4096 | tf_op jit(solution)/shard_map/psum | solution.py:38
  262.6 17.1 %psum.84 = f32[512]{0:T(512)S(1)} all-reduce(f32[512]{0:T(512)S(1)} %fusion.3), channel_id=1, replica_groups=mesh['row'=8,'col'=4] {'row'}, use_global_device_ids=true, to_apply=%region_13.14 | all-reduce | flops 512 | bytes 4096 | tf_op jit(solution)/shard_map/psum | solution.py:41
  280.4 6.3 fusion.6
  286.6 19.3 %all-reduce.1 = (f32[512]{0:T(512)S(1)}, f32[512]{0:T(512)S(1)}) all-reduce(f32[512]{0:T(512)S(1)} %get-tuple-element.29, f32[512]{0:T(512)S(1)} %get-tuple-element.28), channel_id=1, replica_groups=mesh['row'=8,'col'=4] {'row'}, use_global_device_ids=true, to_apply=%region_17.18 | all-reduce | flops 1024 | bytes 8192 | tf_op jit(solution)/shard_map/psum | solution.py:85
  305.9 4.5 multiply_convert_fusion.1
  311.7 7.2 fusion.8
  319.0 114.1 %reduce-scatter.3.cloned.1.call-done = f32[1792,512]{1,0:T(8,128)} async-done(((f32[1792,2048]{1,0:T(8,128)}), f32[1792,512]{1,0:T(8,128)}) %reduce-scatter.3.cloned.1.call-update) | async-done | bytes 3670032 | tf_op jit(solution)/shard_map/reduce_scatter | solution.py:100
  433.1 6.8 multiply_add_fusion.1
  439.9 3.7 fusion.5
  443.7 21.3 %all-reduce = (f32[512]{0:T(512)S(1)}, f32[512]{0:T(512)S(1)}) all-reduce(f32[512]{0:T(512)S(1)} %get-tuple-element.27, f32[512]{0:T(512)S(1)} %get-tuple-element.26), channel_id=1, replica_groups=mesh['row'=8,'col'=4] {'row'}, use_global_device_ids=true, to_apply=%region_22.23 | all-reduce | flops 1024 | bytes 8192 | tf_op jit(solution)/shard_map/psum | solution.py:85
  465.0 4.7 multiply_convert_fusion
  469.7 7.3 fusion.9
  478.5 9.9 %fusion.11 = f32[2048,512]{1,0:T(8,128)} fusion(bf16[1792,2048]{1,0:T(8,128)(2,1)} %copy-done.3, bf16[1792,512]{1,0:T(8,128)(2,1)S(1)} %copy-done.7), kind=kOutput, calls=%fused_computation.52 | convolution fusion | flops 3758096384 | bytes 13369344 | tf_op jit(solution)/shard_map/dot_general | solution.py:93
  488.4 10.5 %fusion.10 = f32[2048,512]{1,0:T(8,128)} fusion(bf16[1792,2048]{1,0:T(8,128)(2,1)} %copy-done.4, bf16[1792,512]{1,0:T(8,128)(2,1)S(1)} %copy-done.9), kind=kOutput, calls=%fused_computation.51 | convolution fusion | flops 3758096384 | bytes 13369344 | tf_op jit(solution)/shard_map/dot_general | solution.py:93
  498.9 87.5 %reduce-scatter.5.cloned.1.call-done = f32[1792,512]{1,0:T(8,128)} async-done(((f32[1792,2048]{1,0:T(8,128)}), f32[1792,512]{1,0:T(8,128)}) %reduce-scatter.5.cloned.1.call-update) | async-done | bytes 3670032 | tf_op jit(solution)/shard_map/reduce_scatter | solution.py:100
  586.4 8.5 multiply_add_fusion
  594.9 267.3 %all-reduce.6.cloned.1.call-done = (f32[2048,512]{1,0:T(8,128)}, f32[2048,512]{1,0:T(8,128)}) async-done(((f32[2048,512]{1,0:T(8,128)}, f32[2048,512]{1,0:T(8,128)}), (f32[2048,512]{1,0:T(8,128)}, f32[2048,512]{1,0:T(8,128)})) %all-reduce.6.cloned.1.call-update) | async-done | bytes 8388624 | tf_op jit(solution)/shard_map/psum | solution.py:96
  862.2 4.8 copy.47
  (137 shorter events, 61.3 us)
Async XLA Ops:
  7.2 227.2 %copy-start = (bf16[2048,512]{1,0:T(8,128)(2,1)S(1)}, bf16[2048,512]{1,0:T(8,128)(2,1)}, u32[]{:S(2)}) copy-start(bf16[2048,512]{1,0:T(8,128)(2,1)} %param.18) | copy-start | bytes 6291460
  7.2 425.9 %reduce-scatter.3.cloned.1.call-start = ((), (), s32[]{:S(2)}) async-start(), calls=%async_computation.2 | async-start | bytes 18350080 | tf_op jit(solution)/shard_map/reduce_scatter | solution.py:100
  41.8 50.2 %copy-start.10 = (s32[1792]{0:T(1024)S(1)}, s32[1792]{0:T(1024)}, u32[]{:S(2)}) copy-start(s32[1792]{0:T(1024)} %param.14) | copy-start | bytes 21508
  48.8 40.6 %collective-permute-start = (bf16[1792,512]{1,0:T(8,128)(2,1)}, bf16[1792,512]{1,0:T(8,128)(2,1)}, u32[]{:S(2)}, u32[]{:S(2)}) collective-permute-start(bf16[1792,512]{1,0:T(8,128)(2,1)} %bitcast.6), channel_id=1, source_target_pairs={{0,1},{1,2},{2,3},{3,0},{4,5},{5,6},{6,7},{7,4},{8,9},{9,10},{10,1... | collective-permute-start | bytes 5505032 | tf_op jit(solution)/shard_map/ppermute | solution.py:59
  49.2 47.9 %collective-permute-start.1 = (bf16[1792,512]{1,0:T(8,128)(2,1)}, bf16[1792,512]{1,0:T(8,128)(2,1)}, u32[]{:S(2)}, u32[]{:S(2)}) collective-permute-start(bf16[1792,512]{1,0:T(8,128)(2,1)} %bitcast.6), channel_id=1, source_target_pairs={{0,3},{1,0},{2,1},{3,2},{4,7},{5,4},{6,5},{7,6},{8,11},{9,8},{10,9... | collective-permute-start | bytes 5505032 | tf_op jit(solution)/shard_map/ppermute | solution.py:67
  89.4 23.0 %collective-permute-start.2 = (bf16[1792,512]{1,0:T(8,128)(2,1)}, bf16[1792,512]{1,0:T(8,128)(2,1)}, u32[]{:S(2)}, u32[]{:S(2)}) collective-permute-start(bf16[1792,512]{1,0:T(8,128)(2,1)} %collective-permute-done), channel_id=1, source_target_pairs={{0,1},{1,2},{2,3},{3,0},{4,5},{5,6},{6,7},{7,4},{8,9},{9,10},{10,1... | collective-permute-start | bytes 5505032 | tf_op jit(solution)/shard_map/ppermute | solution.py:59
  97.1 17.0 %copy-start.19 = (bf16[2048,512]{1,0:T(8,128)(2,1)S(1)}, bf16[2048,512]{1,0:T(8,128)(2,1)}, u32[]{:S(2)}) copy-start(bf16[2048,512]{1,0:T(8,128)(2,1)} %param.15) | copy-start | bytes 6291460
  114.2 5.8 copy-start.4
  120.0 45.2 %copy-start.11 = (f32[512]{0:T(512)S(1)}, f32[512]{0:T(512)}, u32[]{:S(2)}) copy-start(f32[512]{0:T(512)} %param.16) | copy-start | bytes 6148
  120.0 45.2 %copy-start.13 = (f32[512]{0:T(512)S(1)}, f32[512]{0:T(512)}, u32[]{:S(2)}) copy-start(f32[512]{0:T(512)} %param.17) | copy-start | bytes 6148
  172.0 39.4 %collective-permute-start.3 = (bf16[1792,512]{1,0:T(8,128)(2,1)S(1)}, bf16[1792,512]{1,0:T(8,128)(2,1)S(1)}, u32[]{:S(2)}, u32[]{:S(2)}) collective-permute-start(bf16[1792,512]{1,0:T(8,128)(2,1)S(1)} %bitcast.48), channel_id=1, source_target_pairs={{0,1},{1,2},{2,3},{3,0},{4,5},{5,6},{6,7},{7,4},{8,9},{9,10},{10,1... | collective-permute-start | bytes 5505032 | tf_op jit(solution)/shard_map/ppermute | solution.py:59
  172.1 43.8 %collective-permute-start.4 = (bf16[1792,512]{1,0:T(8,128)(2,1)S(1)}, bf16[1792,512]{1,0:T(8,128)(2,1)S(1)}, u32[]{:S(2)}, u32[]{:S(2)}) collective-permute-start(bf16[1792,512]{1,0:T(8,128)(2,1)S(1)} %bitcast.49), channel_id=1, source_target_pairs={{0,3},{1,0},{2,1},{3,2},{4,7},{5,4},{6,5},{7,6},{8,11},{9,8},{10,9... | collective-permute-start | bytes 5505032 | tf_op jit(solution)/shard_map/ppermute | solution.py:67
  211.4 22.7 %collective-permute-start.5 = (bf16[1792,512]{1,0:T(8,128)(2,1)S(1)}, bf16[1792,512]{1,0:T(8,128)(2,1)S(1)}, u32[]{:S(2)}, u32[]{:S(2)}) collective-permute-start(bf16[1792,512]{1,0:T(8,128)(2,1)S(1)} %collective-permute-done.3), channel_id=1, source_target_pairs={{0,1},{1,2},{2,3},{3,0},{4,5},{5,6},{6,7},{7,4},{8,9},{9,10},{10,1... | collective-permute-start | bytes 5505032 | tf_op jit(solution)/shard_map/ppermute | solution.py:59
  234.4 5.8 copy-start.3
  240.2 40.1 %copy-start.12 = (f32[512]{0:T(512)S(1)}, f32[512]{0:T(512)}, u32[]{:S(2)}) copy-start(f32[512]{0:T(512)} %param.19) | copy-start | bytes 6148
  240.2 40.1 %copy-start.14 = (f32[512]{0:T(512)S(1)}, f32[512]{0:T(512)}, u32[]{:S(2)}) copy-start(f32[512]{0:T(512)} %param.20) | copy-start | bytes 6148
  305.9 4.5 copy-start.15
  305.9 4.6 copy-start.17
  310.5 1.2 copy-start.6
  319.0 267.5 %reduce-scatter.5.cloned.1.call-start = ((), (), s32[]{:S(2)}) async-start(), calls=%async_computation.3 | async-start | bytes 18350080 | tf_op jit(solution)/shard_map/reduce_scatter | solution.py:100
  433.1 6.8 copy-start.2
  465.0 4.7 copy-start.16
  465.0 4.7 copy-start.18
  465.0 4.7 copy-start.20
  469.7 7.3 copy-start.8
  477.0 1.5 copy-start.7
  477.0 385.2 %all-reduce.6.cloned.1.call-start = ((), (), s32[]{:S(2)}) async-start(), calls=%async_computation.4 | async-start | bytes 16777216 | tf_op jit(solution)/shard_map/psum | solution.py:96
  478.5 9.9 %copy-start.9 = (bf16[1792,512]{1,0:T(8,128)(2,1)S(1)}, bf16[1792,512]{1,0:T(8,128)(2,1)}, u32[]{:S(2)}) copy-start(bf16[1792,512]{1,0:T(8,128)(2,1)} %copy-done.8) | copy-start | bytes 5505028
  862.2 4.8 copy-start.5
  862.2 6.8 copy-start.1
Sparse Core Ops, SparseCore 0:
  319.1 113.9 reduce-scatter.2
  477.1 109.2 reduce-scatter.4
  591.1 271.0 all-reduce.5
